TPU v7x, 32 devices: a whole 2x2x4 slice. The times are simulated.
32 devices in a mesh: row: 8 (over z, core), col: 4 (over y, x).
Axes of the slice: x: 2, y: 2, z: 4, core: 2. Of those that a mesh axis runs over, the one named last changes fastest.
Arguments:
- amplitudes: bfloat16 [16, 16, 800, 800], P('col', None, 'row'), as said below
- integrals: bfloat16 [16, 16, 800, 800], P('col', None, 'row'), may hold values from -6 to 6
- fock_virtual: bfloat16 [800, 800], replicated, may hold values from -0.21875 to 0.21875
- occ_levels: int32 [16], replicated, may hold values from -12 to -3
- vir_levels: int32 [800], replicated, may hold values from 2 to 21
- ladder_ints: bfloat16 [800, 800, 2, 800], P('row', 'col'), may hold values from -0.0078125 to 0.0078125
Outputs:
- new_amps: bfloat16 [16, 16, 800, 800], P('col', None, 'row')
- ladder: bfloat16 [16, 16, 2, 800], P('col', 'row')
Inputs may be any that keep to these rules, and one draw needn't show every extreme that they name: amplitudes[i, j, a, b] equals amplitudes[j, i, b, a] exactly.
All inputs are finite; a program needn't handle non-finite values.
Results may differ from a plain program's by a relative error of at most 0.0049.
Values may be sent and summed in bfloat16 or wider, within the bound.
A program may use at most 384 MiB of HBM per device.

v0:
```python
import jax
import jax.numpy as jnp
from jax import lax
from jax.sharding import PartitionSpec as P

level_step = 0.1


def mirror_pairs(dressed):
    regrouped = lax.all_to_all(
        lax.all_to_all(dressed, "row", split_axis=3, concat_axis=2, tiled=True),
        "col",
        split_axis=1,
        concat_axis=0,
        tiled=True,
    )
    return jnp.transpose(regrouped, (1, 0, 3, 2))


def body(amplitudes, integrals, fock_virtual, occ_levels, vir_levels, ladder_ints):
    occ_block, occ_all, vir_block, vir_all = amplitudes.shape
    right_term = jnp.einsum(
        "ijac,bc->ijab", amplitudes, fock_virtual, preferred_element_type=jnp.float32
    )
    dressed = integrals.astype(jnp.float32) + 2.0 * right_term
    summed = dressed + mirror_pairs(dressed)
    occ_mine = lax.dynamic_slice_in_dim(occ_levels, lax.axis_index("col") * occ_block, occ_block, 0)
    vir_mine = lax.dynamic_slice_in_dim(vir_levels, lax.axis_index("row") * vir_block, vir_block, 0)
    level_sum = (
        vir_mine[None, None, :, None]
        + vir_levels[None, None, None, :]
        - occ_mine[:, None, None, None]
        - occ_levels[None, :, None, None]
    )
    denom = level_sum.astype(jnp.float32) * level_step
    new_amps = (summed / denom).astype(jnp.bfloat16)
    slab_rows, slab_cols, window_size, vir_width = ladder_ints.shape
    weights = ladder_ints.reshape(slab_rows * slab_cols, window_size * vir_width)
    received = lax.all_to_all(new_amps, "col", split_axis=3, concat_axis=0, tiled=True)
    pair_count = received.shape[0] * received.shape[1]
    flat_amps = received.reshape(pair_count, slab_rows * slab_cols)
    product = jnp.dot(flat_amps, weights, preferred_element_type=jnp.float32)
    ladder_term = product.reshape(received.shape[0], received.shape[1], window_size, vir_width)
    partial_sum = lax.psum_scatter(ladder_term, "col", scatter_dimension=0, tiled=True)
    ladder = lax.psum_scatter(partial_sum, "row", scatter_dimension=1, tiled=True)
    return (new_amps, ladder.astype(jnp.bfloat16))


def solution(mesh):
    placed = (
        P("col", None, "row", None),
        P("col", None, "row", None),
        P(),
        P(),
        P(),
        P("row", "col", None, None),
    )
    return jax.shard_map(
        body,
        mesh=mesh,
        in_specs=placed,
        out_specs=(P("col", None, "row", None), P("col", "row", None, None)),
        check_vma=False,
    )
```

profile of v0, /device:TPU:0, one launch (start us, length us, event | category | flops | bytes accessed | tf_op | source)
XLA Modules:
  0.0 1422.8 jit_solution(17913084116485952195)
XLA Ops:
  7.2 1.4 copy-done
  8.5 22.5 %multiply_add_fusion = f32[4,16,100,800]{3,2,1,0:T(8,128)} fusion(bf16[4,16,100,800]{3,1,2,0:T(8,128)(2,1)} %param.7, bf16[4,16,100,800]{3,1,2,0:T(8,128)(2,1)} %param.6, bf16[800,800]{1,0:T(8,128)(2,1)S(1)} %copy-done), kind=kOutput, calls=%fused_computation.1 | convolution fusion | flops 8207360000 | bytes 42240000 | tf_op jit(solution)/shard_map/ijac,bc->ijab/dot_general | solution.py:22
  31.1 30.0 %copy.53 = f32[4,16,100,800]{2,1,0,3:T(8,128)} copy(f32[4,16,100,800]{3,2,1,0:T(8,128)} %multiply_add_fusion) | data formatting | bytes 40960000 | tf_op jit(solution)/shard_map/add | solution.py:25
  61.1 572.2 %all_to_all.51 = f32[4,16,100,800]{2,1,0,3:T(8,128)S(1)} all-to-all(f32[4,16,100,800]{2,1,0,3:T(8,128)} %copy.53), channel_id=1, replica_groups=mesh['row'=8,'col'=4] {'row'}, dimensions={3} | all-to-all | bytes 40960000 | tf_op jit(solution)/shard_map/all_to_all | solution.py:11
  633.3 31.2 %copy.70 = f32[4,16,8,100,100]{3,2,0,4,1:T(8,128)} copy(f32[4,16,8,100,100]{3,1,0,4,2:T(8,128)S(1)} %bitcast.31) | data formatting | bytes 40960000 | tf_op jit(solution)/shard_map/all_to_all | solution.py:11
  664.4 29.7 %reshape.57 = f32[4,16,800,100]{2,0,3,1:T(4,128)} reshape(f32[4,16,8,100,100]{3,2,0,4,1:T(8,128)} %copy.70) | data formatting | bytes 40960000 | tf_op jit(solution)/shard_map/all_to_all | solution.py:11
  694.2 8.3 all-to-all-start.1
  702.5 0.1 dynamic_slice.7
  702.6 0.1 dynamic_slice.6
  702.7 0.1 broadcast_add_fusion
  702.8 0.2 broadcast_subtract_fusion
  703.0 247.5 %all-to-all-done.1 = f32[4,16,800,100]{2,0,3,1:T(4,128)} async-done(((f32[4,16,800,100]{2,0,3,1:T(4,128)}), f32[4,16,800,100]{2,0,3,1:T(4,128)}, u32[]{:S(2)}, u32[]{:S(2)}) %all-to-all-start.1) | async-done | bytes 20480032 | tf_op jit(solution)/shard_map/all_to_all | solution.py:10
  950.5 20.5 %copy.57 = f32[4,16,800,100]{2,3,1,0:T(8,128)} copy(f32[4,16,800,100]{2,0,3,1:T(4,128)} %all-to-all-done.1) | data formatting | bytes 40960000 | tf_op jit(solution)/shard_map/all_to_all | solution.py:10
  971.0 21.5 %copy.58 = f32[4,4,4,800,100]{3,4,1,0,2:T(8,128)} copy(f32[4,4,4,800,100]{3,4,2,0,1:T(8,128)} %bitcast.35) | data formatting | bytes 40960000 | tf_op jit(solution)/shard_map/all_to_all | solution.py:10
  992.5 1.1 slice-done.4
  993.6 0.8 slice-done.5
  994.4 16.5 %divide_convert_fusion = bf16[4,16,100,800]{3,2,1,0:T(8,128)(2,1)} fusion(f32[4,16,100,800]{3,2,1,0:T(8,128)S(1)} %bitcast.33, f32[4,16,100,800]{3,2,1,0:T(8,128)} %bitcast.34, s32[16]{0:T(128)S(1)} %copy-done.3, s32[4,100,800]{2,1,0:T(8,128)S(1)} %broadcast_subtract_fusion), kind=kLoop, calls=%fused_computation | loop fusion | flops 30720000 | bytes 52480064 | tf_op jit(solution)/shard_map/convert_element_type | solution.py:36
  1010.9 22.4 %copy.59 = bf16[4,16,100,800]{2,1,0,3:T(8,128)(2,1)} copy(bf16[4,16,100,800]{3,2,1,0:T(8,128)(2,1)} %divide_convert_fusion) | data formatting | bytes 20480000 | tf_op jit(solution)/shard_map/convert_element_type | solution.py:36
  1033.3 6.4 all-to-all-start.2
  1039.7 0.0 reduce-scatter.2.cloned.1.call-start
  1039.8 137.0 %reshape.53 = bf16[20000,1600]{1,0:T(8,128)(2,1)} reshape(bf16[100,200,2,800]{3,2,1,0:T(2,128)(2,1)} %param.11) | data formatting | bytes 128000000 | tf_op jit(solution)/shard_map/reshape | solution.py:38
  1176.7 79.9 %copy.62 = bf16[1600,20000]{1,0:T(8,128)(2,1)} copy(bf16[1600,20000]{0,1:T(8,128)(2,1)} %bitcast.30) | data formatting | bytes 128000000 | tf_op jit(solution)/shard_map/dot_general | solution.py:42
  1256.6 27.8 %copy.71 = bf16[4,16,100,4,200]{4,3,1,2,0:T(4,128)(2,1)} copy(bf16[4,16,100,4,200]{2,1,0,4,3:T(8,128)(2,1)} %bitcast.9) | data formatting | bytes 20480000 | tf_op jit(solution)/shard_map/all_to_all | solution.py:39
  1284.4 13.7 copy.61
  1298.2 19.6 %reshape.55 = bf16[16,16,20000,1]{2,1,0,3:T(8,128)(2,1)} reshape(bf16[4,4,16,100,200]{4,3,2,1,0:T(8,128)(2,1)} %copy.61) | data formatting | bytes 20480000 | tf_op jit(solution)/shard_map/dot_general | solution.py:42
  1317.7 29.1 %fusion.2 = f32[16,16,2,800]{3,1,2,0:T(8,128)} fusion(bf16[2,800,20000,1]{2,1,0,3:T(8,128)(2,1)} %bitcast.36, bf16[16,16,20000,1]{2,1,0,3:T(8,128)(2,1)} %reshape.55), kind=kOutput, calls=%fused_computation.4 | convolution fusion | flops 16384000000 | bytes 75878400 | tf_op jit(solution)/shard_map/dot_general | solution.py:42
  1346.9 0.6 dynamic-slice
  1348.1 9.9 copy.64
  1358.0 21.9 %reduce-scatter.2.cloned.1.call-done = f32[4,16,2,800]{3,1,2,0:T(8,128)} async-done(((f32[16,16,2,800]{3,1,2,0:T(8,128)}), f32[4,16,2,800]{3,1,2,0:T(8,128)}) %reduce-scatter.2.cloned.1.call-update) | async-done | bytes 409616 | tf_op jit(solution)/shard_map/reduce_scatter | solution.py:44
  1380.0 1.3 copy.63
  1381.3 34.0 %all-reduce.2 = bf16[4,16,2,800]{3,0,2,1:T(4,128)(2,1)S(1)} all-reduce(f32[4,16,2,800]{3,0,2,1:T(4,128)S(1)} %copy.63), channel_id=3, replica_groups=mesh['row'=8,'col'=4] {'row'}, use_global_device_ids=true, to_apply=%region_1.0.clone | all-reduce | flops 102400 | bytes 614400
  1415.3 0.6 copy.65
  (23 shorter events, 0.1 us)
Async XLA Ops:
  7.2 1.4 copy-start
  694.2 8.4 copy-start.3
  694.2 8.5 copy-start.2
  694.2 256.3 %all-to-all-start.1 = ((f32[4,16,800,100]{2,0,3,1:T(4,128)}), f32[4,16,800,100]{2,0,3,1:T(4,128)}, u32[]{:S(2)}, u32[]{:S(2)}) async-start(f32[4,16,800,100]{2,0,3,1:T(4,128)} %reshape.57), calls=%async_computation.1 | async-start | bytes 45875200 | tf_op jit(solution)/shard_map/all_to_all | solution.py:10
  971.0 21.5 %slice-start = ((s8[23855104]{0:T(1024)(128)(4,1)}), s8[4194304]{0:T(1024)(128)(4,1)S(1)}, s32[]{:S(2)}) async-start(s8[23855104]{0:T(1024)(128)(4,1)} %bitcast.32), calls=%async_computation.5 | async-start | bytes 8388608
  971.0 21.5 %slice-start.1 = ((s8[23855104]{0:T(1024)(128)(4,1)}), s8[4194304]{0:T(1024)(128)(4,1)S(1)}, s32[]{:S(2)}) async-start(s8[23855104]{0:T(1024)(128)(4,1)} %bitcast.32), calls=%async_computation.6 | async-start | bytes 8388608
  971.0 21.5 %slice-start.2 = ((s8[23855104]{0:T(1024)(128)(4,1)}), s8[4194304]{0:T(1024)(128)(4,1)S(1)}, s32[]{:S(2)}) async-start(s8[23855104]{0:T(1024)(128)(4,1)} %bitcast.32), calls=%async_computation.7 | async-start | bytes 8388608
  971.0 21.5 %slice-start.3 = ((s8[23855104]{0:T(1024)(128)(4,1)}), s8[4194304]{0:T(1024)(128)(4,1)S(1)}, s32[]{:S(2)}) async-start(s8[23855104]{0:T(1024)(128)(4,1)} %bitcast.32), calls=%async_computation.8 | async-start | bytes 8388608
  971.0 22.6 %slice-start.4 = ((s8[23855104]{0:T(1024)(128)(4,1)}), s8[4194304]{0:T(1024)(128)(4,1)S(1)}, s32[]{:S(2)}) async-start(s8[23855104]{0:T(1024)(128)(4,1)} %bitcast.32), calls=%async_computation.9 | async-start | bytes 8388608
  971.0 23.4 %slice-start.5 = ((s8[23855104]{0:T(1024)(128)(4,1)}), s8[2883584]{0:T(1024)(128)(4,1)S(1)}, s32[]{:S(2)}) async-start(s8[23855104]{0:T(1024)(128)(4,1)} %bitcast.32), calls=%async_computation.10 | async-start | bytes 5767168
  1033.3 223.3 %all-to-all-start.2 = ((bf16[4,16,100,800]{2,1,0,3:T(8,128)(2,1)}), bf16[4,16,100,800]{2,1,0,3:T(8,128)(2,1)}, u32[]{:S(2)}, u32[]{:S(2)}) async-start(bf16[4,16,100,800]{2,1,0,3:T(8,128)(2,1)} %copy.59), calls=%async_computation.2 | async-start | bytes 26214400 | tf_op jit(solution)/shard_map/all_to_all | solution.py:39
  1039.7 340.2 %reduce-scatter.2.cloned.1.call-start = ((), (), s32[]{:S(2)}) async-start(), calls=%async_computation.4 | async-start | bytes 2293760 | tf_op jit(solution)/shard_map/reduce_scatter | solution.py:44
  1317.7 29.2 %copy-start.4 = (u32[32]{0:T(128)S(1)}, u32[32]{0:T(128)}, u32[]{:S(2)}) copy-start(u32[32]{0:T(128)} %constant.28) | copy-start | bytes 388
  1317.7 98.2 %copy-start.1 = (bf16[800,800]{1,0:T(8,128)(2,1)S(1)}, bf16[800,800]{1,0:T(8,128)(2,1)}, u32[]{:S(2)}) copy-start(bf16[800,800]{1,0:T(8,128)(2,1)} %param.8) | copy-start | bytes 3840004
Sparse Core Ops, SparseCore 0:
  1347.0 32.9 reduce-scatter.1
where the time goes:
time: 1430 us; the launch traced here: 1420 us
  blocking collectives  606 us (42%)
  local copies, waits for them, and re-layouts  449 us (31%)
  waiting for transfers between devices  269 us (19%)
  matrix products  51.7 us (4%)
  other arithmetic  16.7 us (1%)
  starting transfers between devices  14.8 us (1%)
  between operations  14.8 us (1%)
    all_to_all x1, blocking collectives, mirror_pairs(): lax.all_to_all(dressed, 'row', split_axis=3, concat_axis=2, tiled=True)  572 us
    all_to_all x1, waiting for transfers between devices, mirror_pairs(): lax.all_to_all(lax.all_to_all(dressed, 'row', split_axis=3, concat_axis=2...  248 us
    reshape x1, local copies, waits for them, and re-layouts, body(): ladder_ints.reshape(slab_rows * slab_cols, window_size * vir_width)  137 us
    dot_general x2, local copies, waits for them, and re-layouts, body(): product = jnp.dot(flat_amps, weights, preferred_element_type=jnp.float32)  99.4 us
    all_to_all x2, local copies, waits for them, and re-layouts, mirror_pairs(): lax.all_to_all(dressed, 'row', split_axis=3, concat_axis=2, tiled=True)  60.9 us
    all_to_all x2, local copies, waits for them, and re-layouts, mirror_pairs(): lax.all_to_all(lax.all_to_all(dressed, 'row', split_axis=3, concat_axis=2...  42 us
    all_to_all x2, local copies, waits for them, and re-layouts, body(): lax.all_to_all(new_amps, 'col', split_axis=3, concat_axis=0, tiled=True)  41.6 us
    unnamed x1, blocking collectives  34 us
  transfers between devices with their start and end apart: 3, of which 2 were waited for; matrix products, arithmetic and copies ran while one was open for 16% of the time, Pallas kernels for 0%

commit v1 on v0

v1 whole, which is shorter than its diff:
```python
import functools

import jax
import jax.numpy as jnp
from jax import lax
from jax.experimental import pallas as pl
from jax.experimental.pallas import tpu as pltpu
from jax.sharding import PartitionSpec as P

level_step = 0.1
MESH = pl.DeviceIdType.MESH


def exchange_kernel(rows, cols, src, dst, send_sem, recv_sem, local_sem):
    count = rows * cols
    me = lax.axis_index("row") * cols + lax.axis_index("col")
    barrier = pltpu.get_barrier_semaphore()

    def place(number):
        return (number // cols, number % cols)

    def greet(k, carry):
        peer = lax.rem(me + k, count)
        pl.semaphore_signal(barrier, inc=1, device_id=place(peer), device_id_type=MESH)
        return carry

    lax.fori_loop(1, count, greet, 0)
    pl.semaphore_wait(barrier, count - 1)
    own = pltpu.make_async_copy(src.at[me], dst.at[me], local_sem)
    own.start()

    def copy_to(k):
        peer = lax.rem(me + k, count)
        return pltpu.make_async_remote_copy(
            src_ref=src.at[peer],
            dst_ref=dst.at[me],
            send_sem=send_sem.at[k - 1],
            recv_sem=recv_sem.at[k - 1],
            device_id=place(peer),
            device_id_type=MESH,
        )

    def begin(k, carry):
        copy_to(k).start()
        return carry

    def finish(k, carry):
        copy_to(k).wait()
        return carry

    lax.fori_loop(1, count, begin, 0)
    lax.fori_loop(1, count, finish, 0)
    own.wait()


def exchange(blocks, rows, cols, number):
    count = rows * cols
    return pl.pallas_call(
        functools.partial(exchange_kernel, rows, cols),
        out_shape=jax.ShapeDtypeStruct(blocks.shape, blocks.dtype),
        in_specs=[pl.BlockSpec(memory_space=pl.ANY)],
        out_specs=pl.BlockSpec(memory_space=pl.ANY),
        scratch_shapes=[
            pltpu.SemaphoreType.DMA((count - 1,)),
            pltpu.SemaphoreType.DMA((count - 1,)),
            pltpu.SemaphoreType.DMA,
        ],
        compiler_params=pltpu.CompilerParams(collective_id=number, has_side_effects=True),
    )(blocks)


def wire_shape(elements):
    lanes = 128
    while elements % lanes:
        lanes //= 2
    return (elements // lanes, lanes)


def mirror_pairs(sent, rows, cols):
    occ_block, occ_all, vir_block, vir_all = sent.shape
    count = rows * cols
    split = sent.reshape(occ_block, cols, occ_block, vir_block, rows, vir_block)
    blocks = jnp.transpose(split, (4, 1, 2, 5, 0, 3))
    elements = blocks.size // count
    received = exchange(blocks.reshape((count,) + wire_shape(elements)), rows, cols, 0)
    received = received.reshape(rows, cols, occ_block, vir_block, occ_block, vir_block)
    return jnp.transpose(received, (2, 1, 4, 3, 0, 5)).reshape(sent.shape)


def body(rows, cols, amplitudes, integrals, fock_virtual, occ_levels, vir_levels, ladder_ints):
    occ_block, occ_all, vir_block, vir_all = amplitudes.shape
    right_term = jnp.einsum(
        "ijac,bc->ijab", amplitudes, fock_virtual, preferred_element_type=jnp.float32
    )
    dressed = integrals.astype(jnp.float32) + 2.0 * right_term
    sent = dressed.astype(jnp.bfloat16)
    summed = dressed + mirror_pairs(sent, rows, cols).astype(jnp.float32)
    occ_mine = lax.dynamic_slice_in_dim(occ_levels, lax.axis_index("col") * occ_block, occ_block, 0)
    vir_mine = lax.dynamic_slice_in_dim(vir_levels, lax.axis_index("row") * vir_block, vir_block, 0)
    level_sum = (
        vir_mine[None, None, :, None]
        + vir_levels[None, None, None, :]
        - occ_mine[:, None, None, None]
        - occ_levels[None, :, None, None]
    )
    denom = level_sum.astype(jnp.float32) * level_step
    new_amps = (summed / denom).astype(jnp.bfloat16)
    slab_rows, slab_cols, window_size, vir_width = ladder_ints.shape
    depth = slab_rows * slab_cols
    pieces = new_amps.reshape(occ_block * occ_all, vir_block, cols, slab_cols)
    pieces = jnp.transpose(pieces, (2, 0, 1, 3)).reshape(cols * occ_block * occ_all, depth)
    received = lax.all_to_all(pieces, "col", split_axis=0, concat_axis=0, tiled=True)
    terms = [
        jnp.dot(
            received,
            ladder_ints[:, :, w, :].reshape(depth, vir_width),
            preferred_element_type=jnp.float32,
        )
        for w in range(window_size)
    ]
    occ_row = occ_all // rows
    term = jnp.stack(terms, axis=1).reshape(cols, occ_block, rows, occ_row, window_size, vir_width)
    term = jnp.transpose(term, (2, 0, 1, 3, 4, 5))
    elements = term.size // (rows * cols)
    parts = exchange(term.reshape((rows * cols,) + wire_shape(elements)), rows, cols, 1)
    ladder = jnp.sum(parts, axis=0).reshape(occ_block, occ_row, window_size, vir_width)
    return (new_amps, ladder.astype(jnp.bfloat16))


def solution(mesh):
    placed = (
        P("col", None, "row", None),
        P("col", None, "row", None),
        P(),
        P(),
        P(),
        P("row", "col", None, None),
    )
    return jax.shard_map(
        functools.partial(body, mesh.shape["row"], mesh.shape["col"]),
        mesh=mesh,
        in_specs=placed,
        out_specs=(P("col", None, "row", None), P("col", "row", None, None)),
        check_vma=False,
    )
```

time: 1430 us -> 911 us (0.64)
  the two profiles are of different devices: /device:TPU:0 before, /device:TPU:15 now
where the time goes in v1:
time: 911 us; the launch traced here: 900 us
  local copies, waits for them, and re-layouts  489 us (54%)
  Pallas kernels  304 us (33%)
  matrix products  72.7 us (8%)
  other arithmetic  27.1 us (3%)
    pallas_call x2, Pallas kernels, exchange(): pl.pallas_call(functools.partial(exchange_kernel, rows, cols), out_shape=...  304 us
    slice x1, local copies, waits for them, and re-layouts, body(): ladder_ints[:, :, w, :].reshape(depth, vir_width)  133 us
    convert_element_type x3, local copies, waits for them, and re-layouts, body(): summed = dressed + mirror_pairs(sent, rows, cols).astype(jnp.float32)  111 us
    unnamed x9, local copies, waits for them, and re-layouts  81.8 us
    dot_general x2, matrix products, body(): jnp.dot(received, ladder_ints[:, :, w, :].reshape(depth, vir_width), pref...  47.1 us
    reshape x1, local copies, waits for them, and re-layouts, mirror_pairs(): blocks.reshape((count,) + wire_shape(elements))  41.6 us
    all_to_all x2, local copies, waits for them, and re-layouts, body(): lax.all_to_all(pieces, 'col', split_axis=0, concat_axis=0, tiled=True)  32 us
    reshape x1, local copies, waits for them, and re-layouts, body(): pieces = new_amps.reshape(occ_block * occ_all, vir_block, cols, slab_cols)  28.2 us
  transfers between devices with their start and end apart: 1, of which 0 were waited for; matrix products, arithmetic and copies ran while one was open for 24% of the time, Pallas kernels for 0%

profile of v1, /device:TPU:15, one launch (start us, length us, event | category | flops | bytes accessed | tf_op | source)
XLA Modules:
  0.0 900.4 jit_solution(12087190860197950798)
XLA Ops:
  0.6 0.0 copy-start
  0.7 0.9 dynamic_slice.6
  1.5 0.8 broadcast_add_fusion
  2.3 25.6 %fusion = (bf16[4,16,100,800]{3,2,1,0:T(8,128)(2,1)}, f32[4,16,100,800]{3,2,1,0:T(8,128)}) fusion(bf16[4,16,100,800]{3,1,2,0:T(8,128)(2,1)} %param.7, bf16[800,800]{1,0:T(8,128)(2,1)S(1)} %copy-done, bf16[4,16,100,800]{3,1,2,0:T(8,128)(2,1)} %param.6), kind=kOutput, calls=%fused_computation.2 | convolution fusion | flops 8212480000 | bytes 52480000 | tf_op jit(solution)/shard_map/ijac,bc->ijab/dot_general | solution.py:92
  28.0 24.1 %reshape.94 = bf16[4,4,4,100,8,100]{5,4,3,2,1,0:T(8,128)(2,1)} reshape(bf16[4,16,100,800]{3,2,1,0:T(8,128)(2,1)} %get-tuple-element.8) | data formatting | bytes 20480000 | tf_op jit(solution)/shard_map/reshape | solution.py:82
  52.0 18.8 %copy.19 = bf16[8,4,4,100,4,100]{5,4,3,2,1,0:T(4,128)(2,1)} copy(bf16[8,4,4,100,4,100]{3,0,5,2,1,4:T(8,128)(2,1)} %bitcast.32) | data formatting | bytes 20480000 | tf_op jit(solution)/shard_map/transpose | solution.py:83
  70.8 41.6 %reshape.86.src = bf16[32,1250,128]{2,1,0:T(8,128)(2,1)} reshape(bf16[8,4,4,100,4,100]{5,4,3,2,1,0:T(4,128)(2,1)} %copy.19) | data formatting | bytes 20480000 | tf_op jit(solution)/shard_map/reshape | solution.py:85
  112.4 263.6 %shard_map.77 = bf16[32,1250,128]{2,1,0:T(8,128)(2,1)} custom-call(bf16[32,1250,128]{2,1,0:T(8,128)(2,1)} %reshape.86.src), custom_call_target="tpu_custom_call" | custom-call | tf_op jit(solution)/shard_map/pallas_call | solution.py:58
  376.0 57.1 %reshape.90 = f32[8,4,4,100,4,100]{5,4,3,2,1,0:T(4,128)} reshape(bf16[32,1250,128]{2,1,0:T(8,128)(2,1)} %shard_map.77) | data formatting | bytes 30720000 | tf_op jit(solution)/shard_map/convert_element_type | solution.py:97
  433.2 26.1 %copy.40 = f32[4,4,4,100,8,100]{5,4,3,2,1,0:T(8,128)} copy(f32[4,4,4,100,8,100]{5,2,3,0,1,4:T(4,128)} %bitcast.31) | data formatting | bytes 40960000 | tf_op jit(solution)/shard_map/convert_element_type | solution.py:97
  459.3 28.2 %reshape.95 = f32[4,16,100,800]{3,2,1,0:T(8,128)} reshape(f32[4,4,4,100,8,100]{5,4,3,2,1,0:T(8,128)} %copy.40) | data formatting | bytes 40960000 | tf_op jit(solution)/shard_map/convert_element_type | solution.py:97
  487.4 0.1 dynamic_slice.7
  487.5 0.2 broadcast_subtract_fusion
  487.7 24.5 %divide_convert_fusion = bf16[4,16,100,800]{3,2,1,0:T(8,128)(2,1)} fusion(f32[4,16,100,800]{3,2,1,0:T(8,128)} %reshape.95, f32[4,16,100,800]{3,2,1,0:T(8,128)} %get-tuple-element.9, s32[16]{0:T(128)S(1)} %copy-done.2, s32[4,100,800]{2,1,0:T(8,128)S(1)} %broadcast_subtract_fusion, bf16[4,16,100,800]{3,1,2,0:T(8,128)(2,1)} %param.7), kind=kLoop, calls=%fused_computation | loop fusion | flops 46080000 | bytes 62720064 | tf_op jit(solution)/shard_map/convert_element_type | solution.py:107
  512.2 28.2 %reshape.96 = bf16[64,100,4,200]{3,2,1,0:T(4,128)(2,1)} reshape(bf16[4,16,100,800]{3,2,1,0:T(8,128)(2,1)} %divide_convert_fusion) | data formatting | bytes 20480000 | tf_op jit(solution)/shard_map/reshape | solution.py:110
  540.4 10.7 %copy.23 = bf16[4,64,100,200]{3,2,1,0:T(8,128)(2,1)} copy(bf16[4,64,100,200]{3,0,2,1:T(4,128)(2,1)} %bitcast.33) | data formatting | bytes 20480000 | tf_op jit(solution)/shard_map/transpose | solution.py:111
  551.1 19.6 %all_to_all.6 = bf16[4,64,20000]{2,1,0:T(8,128)(2,1)} reshape(bf16[4,64,100,200]{3,2,1,0:T(8,128)(2,1)} %copy.23) | data formatting | bytes 20480000 | tf_op jit(solution)/shard_map/all_to_all | solution.py:112
  570.7 6.0 all-to-all-start
  576.6 133.0 %fusion.4 = (bf16[100,200,1,800]{3,2,1,0:T(2,128)(2,1)}, bf16[100,200,1,800]{3,2,1,0:T(2,128)(2,1)}) fusion(bf16[100,200,2,800]{3,2,1,0:T(2,128)(2,1)} %param.11), kind=kLoop, calls=%fused_computation.11 | loop fusion | bytes 128000000 | tf_op jit(solution)/shard_map/slice | solution.py:116
  709.6 9.7 %copy.30 = bf16[4,16,100,800]{3,1,2,0:T(8,128)(2,1)} copy(bf16[4,16,100,800]{3,2,1,0:T(8,128)(2,1)} %divide_convert_fusion) | data formatting | bytes 20480000
  719.4 36.0 %copy.46 = bf16[100,200,1,800]{3,1,2,0:T(8,128)(2,1)} copy(bf16[100,200,1,800]{3,2,1,0:T(2,128)(2,1)} %get-tuple-element.6) | data formatting | bytes 64000000
  755.4 36.0 %copy.47 = bf16[100,200,1,800]{3,1,2,0:T(8,128)(2,1)} copy(bf16[100,200,1,800]{3,2,1,0:T(2,128)(2,1)} %get-tuple-element.7) | data formatting | bytes 64000000
  791.4 12.4 %copy.24 = bf16[4,64,20000]{2,0,1:T(4,128)(2,1)S(1)} copy(bf16[4,64,20000]{2,1,0:T(8,128)(2,1)} %all-to-all-done) | data formatting | bytes 20480000 | tf_op jit(solution)/shard_map/all_to_all | solution.py:112
  803.9 23.0 %fusion.5 = f32[4,4,8,2,800]{4,0,3,2,1:T(4,128)S(1)} fusion(bf16[4,4,8,2,20000]{4,0,3,2,1:T(4,128)(2,1)S(1)} %bitcast.36, bf16[20000,800,1,1,1]{1,0,4,3,2:T(8,128)(2,1)} %bitcast.34), kind=kOutput, calls=%fused_computation.12 | convolution fusion | flops 8192000000 | bytes 43059200 | tf_op jit(solution)/shard_map/dot_general | solution.py:114
  826.9 24.1 %fusion.6 = f32[4,4,8,2,800]{4,0,3,2,1:T(4,128)} fusion(bf16[4,4,8,2,20000]{4,0,3,2,1:T(4,128)(2,1)S(1)} %bitcast.37, bf16[20000,800,1,1,1]{1,0,4,3,2:T(8,128)(2,1)} %bitcast.35), kind=kOutput, calls=%fused_computation.13 | convolution fusion | flops 8192000000 | bytes 43059200 | tf_op jit(solution)/shard_map/dot_general | solution.py:114
  851.0 1.5 copy_bitcast_fusion
  852.5 0.2 maximum_bitcast_fusion
  852.7 1.4 copy.29
  854.1 3.2 reshape.88.src
  857.3 40.3 %shard_map.78 = f32[32,100,128]{2,1,0:T(8,128)} custom-call(f32[32,100,128]{2,1,0:T(8,128)} %reshape.88.src), custom_call_target="tpu_custom_call" | custom-call | tf_op jit(solution)/shard_map/pallas_call | solution.py:58
  897.7 1.6 reduce_sum.9
  899.2 0.7 convert_element_type.39
  (6 shorter events, 0.0 us)
Async XLA Ops:
  0.6 1.7 copy-start
  459.3 28.2 %copy-start.2 = (s32[16]{0:T(128)S(1)}, s32[16]{0:T(128)}, u32[]{:S(2)}) copy-start(s32[16]{0:T(128)} %param.9) | copy-start | bytes 196
  570.7 220.8 %all-to-all-start = ((bf16[4,64,20000]{2,1,0:T(8,128)(2,1)}), bf16[4,64,20000]{2,1,0:T(8,128)(2,1)}, u32[]{:S(2)}, u32[]{:S(2)}) async-start(bf16[4,64,20000]{2,1,0:T(8,128)(2,1)} %all_to_all.6), calls=%async_computation | async-start | bytes 20578304 | tf_op jit(solution)/shard_map/all_to_all | solution.py:112
  826.9 73.1 %copy-start.1 = (bf16[800,800]{1,0:T(8,128)(2,1)S(1)}, bf16[800,800]{1,0:T(8,128)(2,1)}, u32[]{:S(2)}) copy-start(bf16[800,800]{1,0:T(8,128)(2,1)} %param.8) | copy-start | bytes 3840004

commit v2 on v1

--- a/solution.py
+++ b/solution.py
@@ -13,30 +13,30 @@
 
 def exchange_kernel(rows, cols, src, dst, send_sem, recv_sem, local_sem):
     count = rows * cols
-    me = lax.axis_index("row") * cols + lax.axis_index("col")
+    row, col = lax.axis_index("row"), lax.axis_index("col")
+    me = row * cols + col
     barrier = pltpu.get_barrier_semaphore()
 
-    def place(number):
-        return (number // cols, number % cols)
+    def partner(k):
+        turn = k // cols
+        away = rows // 2 + ((turn + 1) // 2) * (1 - 2 * (turn % 2))
+        return ((row + away + rows) % rows, (col + k % cols + 1) % cols)
 
     def greet(k, carry):
-        peer = lax.rem(me + k, count)
-        pl.semaphore_signal(barrier, inc=1, device_id=place(peer), device_id_type=MESH)
+        pl.semaphore_signal(barrier, inc=1, device_id=partner(k), device_id_type=MESH)
         return carry
 
-    lax.fori_loop(1, count, greet, 0)
+    lax.fori_loop(0, count - 1, greet, 0)
     pl.semaphore_wait(barrier, count - 1)
-    own = pltpu.make_async_copy(src.at[me], dst.at[me], local_sem)
-    own.start()
 
     def copy_to(k):
-        peer = lax.rem(me + k, count)
+        peer_row, peer_col = partner(k)
         return pltpu.make_async_remote_copy(
-            src_ref=src.at[peer],
+            src_ref=src.at[peer_row * cols + peer_col],
             dst_ref=dst.at[me],
-            send_sem=send_sem.at[k - 1],
-            recv_sem=recv_sem.at[k - 1],
-            device_id=place(peer),
+            send_sem=send_sem.at[k],
+            recv_sem=recv_sem.at[k],
+            device_id=(peer_row, peer_col),
             device_id_type=MESH,
         )
 
@@ -48,8 +48,10 @@
         copy_to(k).wait()
         return carry
 
-    lax.fori_loop(1, count, begin, 0)
-    lax.fori_loop(1, count, finish, 0)
+    lax.fori_loop(0, count - 1, begin, 0)
+    own = pltpu.make_async_copy(src.at[me], dst.at[me], local_sem)
+    own.start()
+    lax.fori_loop(0, count - 1, finish, 0)
     own.wait()
 
 
@@ -87,6 +89,28 @@
     return jnp.transpose(received, (2, 1, 4, 3, 0, 5)).reshape(sent.shape)
 
 
+def window_kernel(slab_ref, *out_refs):
+    parted = pltpu.einshape("tab->atb", slab_ref[...])
+    for number, out_ref in enumerate(out_refs):
+        out_ref[...] = parted[number]
+
+
+def window_weights(ladder_ints):
+    slab_rows, slab_cols, window_size, vir_width = ladder_ints.shape
+    depth = slab_rows * slab_cols
+    tile = next((t for t in range(400, 0, -8) if depth % t == 0), depth)
+    return pl.pallas_call(
+        window_kernel,
+        grid=(depth // tile,),
+        in_specs=[pl.BlockSpec((tile, window_size, vir_width), lambda k: (k, 0, 0))],
+        out_specs=[pl.BlockSpec((tile, vir_width), lambda k: (k, 0))] * window_size,
+        out_shape=[jax.ShapeDtypeStruct((depth, vir_width), ladder_ints.dtype)] * window_size,
+        cost_estimate=pl.CostEstimate(
+            flops=0, bytes_accessed=4 * ladder_ints.size, transcendentals=0
+        ),
+    )(ladder_ints.reshape(depth, window_size, vir_width))
+
+
 def body(rows, cols, amplitudes, integrals, fock_virtual, occ_levels, vir_levels, ladder_ints):
     occ_block, occ_all, vir_block, vir_all = amplitudes.shape
     right_term = jnp.einsum(
@@ -94,7 +118,8 @@
     )
     dressed = integrals.astype(jnp.float32) + 2.0 * right_term
     sent = dressed.astype(jnp.bfloat16)
-    summed = dressed + mirror_pairs(sent, rows, cols).astype(jnp.float32)
+    mirrored = lax.optimization_barrier(mirror_pairs(sent, rows, cols))
+    summed = dressed + mirrored.astype(jnp.float32)
     occ_mine = lax.dynamic_slice_in_dim(occ_levels, lax.axis_index("col") * occ_block, occ_block, 0)
     vir_mine = lax.dynamic_slice_in_dim(vir_levels, lax.axis_index("row") * vir_block, vir_block, 0)
     level_sum = (
@@ -110,20 +135,19 @@
     pieces = new_amps.reshape(occ_block * occ_all, vir_block, cols, slab_cols)
     pieces = jnp.transpose(pieces, (2, 0, 1, 3)).reshape(cols * occ_block * occ_all, depth)
     received = lax.all_to_all(pieces, "col", split_axis=0, concat_axis=0, tiled=True)
-    terms = [
-        jnp.dot(
-            received,
-            ladder_ints[:, :, w, :].reshape(depth, vir_width),
-            preferred_element_type=jnp.float32,
-        )
-        for w in range(window_size)
-    ]
+    terms = lax.optimization_barrier(
+        [
+            jnp.dot(received, weights, preferred_element_type=jnp.float32)
+            for weights in window_weights(ladder_ints)
+        ]
+    )
     occ_row = occ_all // rows
     term = jnp.stack(terms, axis=1).reshape(cols, occ_block, rows, occ_row, window_size, vir_width)
     term = jnp.transpose(term, (2, 0, 1, 3, 4, 5))
     elements = term.size // (rows * cols)
-    parts = exchange(term.reshape((rows * cols,) + wire_shape(elements)), rows, cols, 1)
-    ladder = jnp.sum(parts, axis=0).reshape(occ_block, occ_row, window_size, vir_width)
+    blocks = term.astype(jnp.bfloat16).reshape((rows * cols,) + wire_shape(elements))
+    parts = exchange(blocks, rows, cols, 1)
+    ladder = jnp.sum(parts.astype(jnp.float32), axis=0).reshape(occ_block, occ_row, window_size, vir_width)
     return (new_amps, ladder.astype(jnp.bfloat16))
 
 

time: 911 us -> 715 us (0.78)
  the two profiles are of different devices: /device:TPU:15 before, /device:TPU:0 now
where the time goes in v2:
time: 715 us; the launch traced here: 709 us
  Pallas kernels  316 us (44%)
  local copies, waits for them, and re-layouts  258 us (36%)
  matrix products  65.1 us (9%)
  waiting for transfers between devices  36.6 us (5%)
  other arithmetic  26.3 us (4%)
    pallas_call x2, Pallas kernels, exchange(): pl.pallas_call(functools.partial(exchange_kernel, rows, cols), out_shape=...  250 us
    pallas_call x1, Pallas kernels, window_weights(): pl.pallas_call(window_kernel, grid=(depth // tile,), in_specs=[pl.BlockSp...  65.5 us
    reshape x1, local copies, waits for them, and re-layouts, mirror_pairs(): received.reshape(rows, cols, occ_block, vir_block, occ_block, vir_block)  51.9 us
    reshape x1, local copies, waits for them, and re-layouts, mirror_pairs(): blocks.reshape((count,) + wire_shape(elements))  41.6 us
    dot_general x2, matrix products, body(): jnp.dot(received, weights, preferred_element_type=jnp.float32)  39.4 us
    all_to_all x1, waiting for transfers between devices, body(): lax.all_to_all(pieces, 'col', split_axis=0, concat_axis=0, tiled=True)  36.6 us
    reshape x1, local copies, waits for them, and re-layouts, body(): pieces = new_amps.reshape(occ_block * occ_all, vir_block, cols, slab_cols)  28.2 us
    dot_general x1, matrix products, body(): jnp.einsum('ijac,bc->ijab', amplitudes, fock_virtual, preferred_element_t...  25.7 us
  transfers between devices with their start and end apart: 1, of which 1 were waited for; matrix products, arithmetic and copies ran while one was open for 1% of the time, Pallas kernels for 9%

profile of v2, /device:TPU:0, one launch (start us, length us, event | category | flops | bytes accessed | tf_op | source)
XLA Modules:
  0.0 708.8 jit_solution(9214724387586320031)
XLA Ops:
  0.7 0.9 dynamic_slice.6
  1.5 0.8 broadcast_add_fusion
  2.3 25.7 %fusion = (bf16[4,16,100,800]{3,2,1,0:T(8,128)(2,1)}, f32[4,16,100,800]{3,2,1,0:T(8,128)}) fusion(bf16[4,16,100,800]{3,1,2,0:T(8,128)(2,1)} %param.7, bf16[800,800]{1,0:T(8,128)(2,1)S(1)} %copy-done, bf16[4,16,100,800]{3,1,2,0:T(8,128)(2,1)} %param.6), kind=kOutput, calls=%fused_computation.2 | convolution fusion | flops 8212480000 | bytes 52480000 | tf_op jit(solution)/shard_map/ijac,bc->ijab/dot_general | solution.py:116
  28.0 24.0 %reshape.86 = bf16[4,4,4,100,8,100]{5,4,3,2,1,0:T(8,128)(2,1)} reshape(bf16[4,16,100,800]{3,2,1,0:T(8,128)(2,1)} %get-tuple-element.14) | data formatting | bytes 20480000 | tf_op jit(solution)/shard_map/reshape | solution.py:84
  52.1 18.8 %copy.18 = bf16[8,4,4,100,4,100]{5,4,3,2,1,0:T(4,128)(2,1)} copy(bf16[8,4,4,100,4,100]{3,0,5,2,1,4:T(8,128)(2,1)} %bitcast.24) | data formatting | bytes 20480000 | tf_op jit(solution)/shard_map/transpose | solution.py:85
  70.9 41.6 %reshape.79.src = bf16[32,1250,128]{2,1,0:T(8,128)(2,1)} reshape(bf16[8,4,4,100,4,100]{5,4,3,2,1,0:T(4,128)(2,1)} %copy.18) | data formatting | bytes 20480000 | tf_op jit(solution)/shard_map/reshape | solution.py:87
  112.5 179.8 %shard_map.77 = bf16[32,1250,128]{2,1,0:T(8,128)(2,1)} custom-call(bf16[32,1250,128]{2,1,0:T(8,128)(2,1)} %reshape.79.src), custom_call_target="tpu_custom_call" | custom-call | tf_op jit(solution)/shard_map/pallas_call | solution.py:60
  292.3 51.9 %reshape.80 = bf16[8,4,4,100,4,100]{5,4,3,2,1,0:T(4,128)(2,1)} reshape(bf16[32,1250,128]{2,1,0:T(8,128)(2,1)} %shard_map.77) | data formatting | bytes 20480000 | tf_op jit(solution)/shard_map/reshape | solution.py:88
  344.2 25.5 %copy.19 = bf16[4,4,4,100,8,100]{5,4,2,1,3,0:T(8,128)(2,1)} copy(bf16[4,4,4,100,8,100]{5,2,3,0,1,4:T(4,128)(2,1)} %bitcast.26) | data formatting | bytes 20480000 | tf_op jit(solution)/shard_map/transpose | solution.py:89
  369.6 21.6 %reshape.81 = bf16[4,16,100,800]{3,1,2,0:T(8,128)(2,1)} reshape(bf16[4,4,4,100,8,100]{5,4,2,1,3,0:T(8,128)(2,1)} %copy.19) | data formatting | bytes 20480000 | tf_op jit(solution)/shard_map/reshape | solution.py:89
  391.3 0.1 dynamic_slice.7
  391.3 0.2 broadcast_subtract_fusion
  391.5 22.7 %divide_convert_fusion = bf16[4,16,100,800]{3,2,1,0:T(8,128)(2,1)} fusion(f32[4,16,100,800]{3,2,1,0:T(8,128)} %get-tuple-element.15, bf16[4,16,100,800]{3,1,2,0:T(8,128)(2,1)} %reshape.81, s32[16]{0:T(128)S(1)} %copy-done.2, s32[4,100,800]{2,1,0:T(8,128)S(1)} %broadcast_subtract_fusion, bf16[4,16,100,800]{3,1,2,0:T(8,128)(2,1)} %param.7), kind=kLoop, calls=%fused_computation | loop fusion | flops 51200000 | bytes 52480064 | tf_op jit(solution)/shard_map/convert_element_type | solution.py:132
  414.2 28.2 %reshape.87 = bf16[64,100,4,200]{3,2,1,0:T(4,128)(2,1)} reshape(bf16[4,16,100,800]{3,2,1,0:T(8,128)(2,1)} %divide_convert_fusion) | data formatting | bytes 20480000 | tf_op jit(solution)/shard_map/reshape | solution.py:135
  442.5 10.7 %copy.22 = bf16[4,64,100,200]{3,2,1,0:T(8,128)(2,1)} copy(bf16[4,64,100,200]{3,0,2,1:T(4,128)(2,1)} %bitcast.25) | data formatting | bytes 20480000 | tf_op jit(solution)/shard_map/transpose | solution.py:136
  453.1 19.6 %all_to_all.8 = bf16[4,64,20000]{2,1,0:T(8,128)(2,1)} reshape(bf16[4,64,100,200]{3,2,1,0:T(8,128)(2,1)} %copy.22) | data formatting | bytes 20480000 | tf_op jit(solution)/shard_map/all_to_all | solution.py:137
  472.7 6.2 all-to-all-start
  478.9 9.7 %copy.26 = bf16[4,16,100,800]{3,1,2,0:T(8,128)(2,1)} copy(bf16[4,16,100,800]{3,2,1,0:T(8,128)(2,1)} %divide_convert_fusion) | data formatting | bytes 20480000
  488.7 65.5 %shard_map.78 = (bf16[20000,800]{1,0:T(8,128)(2,1)}, bf16[20000,800]{1,0:T(8,128)(2,1)}) custom-call(bf16[20000,2,800]{2,1,0:T(2,128)(2,1)} %bitcast.8.slab_ref), custom_call_target="tpu_custom_call" | custom-call | bytes 128000000 | tf_op jit(solution)/shard_map/pallas_call | solution.py:102
  554.1 36.6 %all-to-all-done = bf16[4,64,20000]{2,1,0:T(8,128)(2,1)} async-done(((bf16[4,64,20000]{2,1,0:T(8,128)(2,1)}), bf16[4,64,20000]{2,1,0:T(8,128)(2,1)}, u32[]{:S(2)}, u32[]{:S(2)}) %all-to-all-start) | async-done | bytes 10240032 | tf_op jit(solution)/shard_map/all_to_all | solution.py:137
  590.7 19.5 %fusion.4 = bf16[256,800]{0,1:T(8,128)(2,1)S(1)} fusion(bf16[256,20000]{1,0:T(8,128)(2,1)} %bitcast.7, bf16[20000,800]{1,0:T(8,128)(2,1)} %get-tuple-element.6), kind=kOutput, calls=%fused_computation.9 | convolution fusion | flops 8192000000 | bytes 42649600 | tf_op jit(solution)/shard_map/dot_general | solution.py:140
  610.2 19.9 %fusion.5 = bf16[256,800]{0,1:T(8,128)(2,1)S(1)} fusion(bf16[256,20000]{1,0:T(8,128)(2,1)} %bitcast.7, bf16[20000,800]{1,0:T(8,128)(2,1)} %get-tuple-element.7), kind=kOutput, calls=%fused_computation.10 | convolution fusion | flops 8192000000 | bytes 42649600 | tf_op jit(solution)/shard_map/dot_general | solution.py:140
  630.1 0.2 copy.23
  630.4 0.2 stack.9
  630.6 0.2 copy.24
  630.8 0.2 stack.10
  631.0 1.4 maximum_bitcast_fusion
  632.4 1.4 copy.25
  633.8 2.4 reshape.84.src
  636.2 70.6 %shard_map.79 = bf16[32,100,128]{2,1,0:T(8,128)(2,1)} custom-call(bf16[32,100,128]{2,1,0:T(8,128)(2,1)} %reshape.84.src), custom_call_target="tpu_custom_call" | custom-call | tf_op jit(solution)/shard_map/pallas_call | solution.py:60
  706.8 1.3 reduce_sum.12
  708.1 0.7 convert_element_type.30
  (6 shorter events, 0.0 us)
Async XLA Ops:
  0.6 1.7 copy-start
  369.6 21.6 %copy-start.2 = (s32[16]{0:T(128)S(1)}, s32[16]{0:T(128)}, u32[]{:S(2)}) copy-start(s32[16]{0:T(128)} %param.9) | copy-start | bytes 196
  472.7 118.0 %all-to-all-start = ((bf16[4,64,20000]{2,1,0:T(8,128)(2,1)}), bf16[4,64,20000]{2,1,0:T(8,128)(2,1)}, u32[]{:S(2)}, u32[]{:S(2)}) async-start(bf16[4,64,20000]{2,1,0:T(8,128)(2,1)} %all_to_all.8), calls=%async_computation | async-start | bytes 20578304 | tf_op jit(solution)/shard_map/all_to_all | solution.py:137
  610.2 98.6 %copy-start.1 = (bf16[800,800]{1,0:T(8,128)(2,1)S(1)}, bf16[800,800]{1,0:T(8,128)(2,1)}, u32[]{:S(2)}) copy-start(bf16[800,800]{1,0:T(8,128)(2,1)} %param.8) | copy-start | bytes 3840004
